TPU v7x, 128 devices: a whole 4x4x4 slice. The times are simulated.
128 devices in a mesh: cfg: 2 (over y_hi), group: 16 (over y_lo, x, core), mp: 4 (over z).
Axes of the slice: x: 4, y: 4 (y_hi: 2, y_lo: 2; y = y_hi * 2 + y_lo), z: 4, core: 2. Of those that a mesh axis runs over, the one named last changes fastest.
Arguments:
- latents: float32 [16384, 64], P(('group', 'mp')), may hold values from -0.6 to 0.6
- text_hidden: bfloat16 [2, 8192, 3072], P('cfg', ('group', 'mp')), may hold values from -6 to 6
- w_img_in: bfloat16 [64, 3072], replicated, may hold values from -0.75 to 0.75
- w_img_qkv: bfloat16 [3072, 4608], P(None, 'mp'), may hold values from -1 to 1
- w_txt_kv: bfloat16 [3072, 3072], P(None, 'mp'), may hold values from -0.109375 to 0.109375
- q_gain: float32 [128], replicated, may hold values from 0.25 to 1.75
- k_gain: float32 [128], replicated, may hold values from 0.25 to 1.75
- w_out: bfloat16 [1536, 3072], replicated, may hold values from -1 to 1
- w_final: bfloat16 [3072, 64], replicated, may hold values from -0.109375 to 0.109375
- mod_img: float32 [8, 3, 3072], replicated, may hold values from -3 to 3
- mod_txt: float32 [8, 2, 3072], replicated, may hold values from -3 to 3
- mod_final: float32 [8, 2, 3072], replicated, may hold values from -3 to 3
- guide: float32 [16], replicated, may hold values from 1.5 to 5
- step_size: float32 [8], replicated, may hold values from 0.02 to 0.3
- img_len: int32 [16], replicated, may hold values from 1 to 1024, as said below
- txt_len: int32 [16], replicated, may hold values from 1 to 512, as said below
- split_flag: int32 [2, 16], replicated, may hold values from 0 to 1, as said below
- tstep: int32 [16], replicated, may hold values from 0 to 7
Outputs:
- velocity: float32 [2, 8192, 64], P('cfg', ('group', 'mp'))
- next_latents: float32 [2, 8192, 64], P('cfg', ('group', 'mp'))
Inputs may be any that keep to these rules, and one draw needn't show every extreme that they name: `img_len`: some group has exactly 1024 live image tokens. `txt_len`: some group has exactly 512 live text tokens. `split_flag`: entries [c, 2j] and [c, 2j + 1] are equal; at least one such pair carries 1 and at least one carries 0.
All inputs are finite; a program needn't handle non-finite values.
Results may differ from a plain program's by a relative error of at most 0.035.
Values may be sent and summed in bfloat16 or wider, within the bound.
A program may use at most 192 MiB of HBM per device.

v0:
```python
import jax
import jax.numpy as jnp
from jax import lax
from jax.sharding import PartitionSpec as P

HD = 128


def partner(value, axis, bit):
    mask = 2**bit
    pairs = [(source, source ^ mask) for source in range(lax.axis_size(axis))]
    return lax.ppermute(value, axis, pairs)


def layer_norm(values):
    center = values - jnp.mean(values, -1, keepdims=True)
    spread = jnp.mean(center * center, -1, keepdims=True)
    return center * lax.rsqrt(spread + 1e-06)


def head_norm(values, gain):
    return values * lax.rsqrt(jnp.mean(values * values, -1, keepdims=True) + 1e-06) * gain


def pick_entry(table, index):
    return lax.dynamic_index_in_dim(table, index, 0, keepdims=False)


def local(
    latents,
    text_hidden,
    w_img_in,
    w_img_qkv,
    w_txt_kv,
    q_gain,
    k_gain,
    w_out,
    w_final,
    mod_img,
    mod_txt,
    mod_final,
    guide,
    step_size,
    img_len,
    txt_len,
    split_flag,
    tstep,
):
    group_index = lax.axis_index("group")
    mp_index = lax.axis_index("mp")
    cfg_index = lax.axis_index("cfg")
    mp_count = lax.axis_size("mp")
    mate_index = jnp.bitwise_xor(group_index, 1)
    step_index = pick_entry(tstep, group_index)
    mod_rows = pick_entry(mod_img, step_index)
    text_rows = pick_entry(mod_txt, step_index)
    final_rows = pick_entry(mod_final, step_index)
    shard_rows = latents.shape[0]
    half_rows = shard_rows // 2
    full_img = shard_rows * mp_count
    full_txt = text_hidden.shape[1] * mp_count
    local_heads = w_img_qkv.shape[1] // (3 * HD)
    x_img = jnp.dot(latents.astype(jnp.bfloat16), w_img_in, preferred_element_type=jnp.float32)
    img_mod = (layer_norm(x_img) * (1.0 + mod_rows[1]) + mod_rows[0]).astype(jnp.bfloat16)
    txt_mod = (
        layer_norm(text_hidden[0].astype(jnp.float32)) * (1.0 + text_rows[1]) + text_rows[0]
    ).astype(jnp.bfloat16)
    img_full, txt_full = (
        lax.all_gather(img_mod, "mp", axis=0, tiled=True),
        lax.all_gather(txt_mod, "mp", axis=0, tiled=True),
    )
    qkv = jnp.dot(img_full, w_img_qkv, preferred_element_type=jnp.float32).reshape(
        full_img, local_heads, 3, HD
    )
    query = head_norm(qkv[:, :, 0], q_gain).astype(jnp.bfloat16)
    key_img = head_norm(qkv[:, :, 1], k_gain).astype(jnp.bfloat16)
    value_img = qkv[:, :, 2].astype(jnp.bfloat16)
    text_kv = jnp.dot(txt_full, w_txt_kv, preferred_element_type=jnp.float32).reshape(
        full_txt, local_heads, 2, HD
    )
    key_txt = head_norm(text_kv[:, :, 0], k_gain).astype(jnp.bfloat16)
    value_txt = text_kv[:, :, 1].astype(jnp.bfloat16)
    key_rows = jnp.concatenate([key_txt, key_img], axis=0)
    value_rows = jnp.concatenate([value_txt, value_img], axis=0)
    mate_keys, mate_values = partner((key_rows, value_rows), "group", 0)
    spots_txt = jnp.arange(full_txt, dtype=jnp.int32)
    spots_img = jnp.arange(full_img, dtype=jnp.int32)

    def live_rows(index):
        return jnp.concatenate(
            [spots_txt < pick_entry(txt_len, index), spots_img < pick_entry(img_len, index)]
        )

    flagged = pick_entry(pick_entry(split_flag, cfg_index), group_index) == 1
    live = jnp.concatenate([live_rows(group_index), live_rows(mate_index) & flagged])
    all_keys = jnp.concatenate([key_rows, mate_keys], axis=0)
    all_values = jnp.concatenate([value_rows, mate_values], axis=0)
    scores = jnp.einsum(
        "qhe,khe->hqk", query, all_keys, preferred_element_type=jnp.float32
    ) * HD ** (-0.5)
    scores = jnp.where(live[None, None, :], scores, -1e30)
    weights = jnp.exp(scores - jnp.max(scores, -1, keepdims=True))
    probs = (weights / jnp.sum(weights, -1, keepdims=True)).astype(jnp.bfloat16)
    mixed = jnp.einsum(
        "hqk,khe->qhe", probs, all_values, preferred_element_type=jnp.float32
    ).astype(jnp.bfloat16)
    mixed = mixed.reshape(full_img, local_heads * HD)
    w_local = lax.dynamic_slice_in_dim(w_out, mp_index * local_heads * HD, local_heads * HD, 0)
    attended = lax.psum_scatter(
        jnp.dot(mixed, w_local, preferred_element_type=jnp.float32),
        "mp",
        scatter_dimension=0,
        tiled=True,
    )
    hidden = x_img + mod_rows[2] * attended
    final = (layer_norm(hidden) * (1.0 + final_rows[1]) + final_rows[0]).astype(jnp.bfloat16)
    own_velocity = jnp.dot(final, w_final, preferred_element_type=jnp.float32)
    scale = pick_entry(guide, group_index)
    other_velocity = partner(own_velocity.astype(jnp.bfloat16), "cfg", 0).astype(own_velocity.dtype)
    is_cond = cfg_index == 0
    cond_part = jnp.where(is_cond, own_velocity, other_velocity)
    uncond_part = jnp.where(is_cond, other_velocity, own_velocity)
    guided_all = uncond_part + scale * (cond_part - uncond_part)
    guided = lax.dynamic_slice_in_dim(guided_all, cfg_index * half_rows, half_rows, 0)
    row_place = (
        mp_index * shard_rows + cfg_index * half_rows + jnp.arange(half_rows, dtype=jnp.int32)
    )
    row_live = row_place < pick_entry(img_len, group_index)
    guided = jnp.where(row_live[:, None], guided, 0.0)
    start_rows = lax.dynamic_slice_in_dim(latents, cfg_index * half_rows, half_rows, 0)
    moved = start_rows - pick_entry(step_size, step_index) * guided
    return (guided[None], moved[None])


def solution(mesh):
    placed = (
        P(("group", "mp"), None),
        P("cfg", ("group", "mp"), None),
        P(),
        P(None, "mp"),
        P(None, "mp"),
        P(),
        P(),
        P(),
        P(),
        P(),
        P(),
        P(),
        P(),
        P(),
        P(),
        P(),
        P(),
        P(),
    )
    return jax.shard_map(
        local,
        mesh=mesh,
        in_specs=placed,
        out_specs=(P("cfg", ("group", "mp"), None), P("cfg", ("group", "mp"), None)),
        check_vma=False,
    )
```

profile of v0, /device:TPU:1, one launch (start us, length us, event | category | flops | bytes accessed | tf_op | source)
XLA Modules:
  0.0 342.4 jit_solution(17559711383967402021)
XLA Ops:
  14.3 2.4 fusion.21
  18.8 1.6 constant_dynamic-slice_fusion
  20.3 1.8 add_convert_fusion.1
  25.1 34.8 %all-gather.3.cloned.1.call-done = bf16[512,3072]{1,0:T(8,128)(2,1)} async-done(((bf16[128,3072]{1,0:T(8,128)(2,1)}), bf16[512,3072]{1,0:T(8,128)(2,1)}) %all-gather.3.cloned.1.call-update) | async-done | bytes 3145744 | tf_op jit(solution)/shard_map/all_gather | solution.py:70
  59.9 7.0 %fusion.53 = f32[512,768]{1,0:T(8,128)} fusion(bf16[512,3072]{1,0:T(8,128)(2,1)} %all-gather.3.cloned.1.call-done, bf16[3072,768]{1,0:T(8,128)(2,1)} %param.22), kind=kOutput, calls=%fused_computation.97 | convolution fusion | flops 2415919104 | bytes 9437184 | tf_op jit(solution)/shard_map/dot_general | solution.py:78
  66.9 2.9 reshape.125
  69.8 2.1 slice.60
  72.5 55.0 %all-gather.5.cloned.1.call-done = bf16[1024,3072]{1,0:T(8,128)(2,1)} async-done(((bf16[256,3072]{1,0:T(8,128)(2,1)}), bf16[1024,3072]{1,0:T(8,128)(2,1)}) %all-gather.5.cloned.1.call-update) | async-done | bytes 6291472 | tf_op jit(solution)/shard_map/all_gather | solution.py:69
  127.5 11.3 %fusion.54 = f32[1024,1152]{0,1:T(8,128)S(1)} fusion(bf16[1024,3072]{1,0:T(8,128)(2,1)} %all-gather.5.cloned.1.call-done, bf16[3072,1152]{1,0:T(8,128)(2,1)} %param.21), kind=kOutput, calls=%fused_computation.98 | convolution fusion | flops 7247757312 | bytes 18087936 | tf_op jit(solution)/shard_map/dot_general | solution.py:72
  138.8 2.1 copy-done.2
  142.2 3.0 copy.40
  145.2 1.9 fusion.22
  147.1 1.9 fusion.24
  154.9 3.1 slice.57
  158.0 2.9 copy.41
  163.3 2.1 pad_maximum_fusion.1
  165.4 1.6 multiply_reduce_fusion.2
  167.0 19.6 %fusion.51 = (f32[3,1024]{1,0:T(4,128)}, f32[3,1024,3072]{2,1,0:T(8,128)}) fusion(pred[3072]{0:T(1024)(128)(4,1)} %pad_add_fusion, bf16[1536,3,128]{2,0,1:T(8,128)(2,1)} %collective-permute-done.1, bf16[1024,3,128]{2,0,1:T(8,128)(2,1)} %copy-done.4, bf16[512,3,128]{2,0,1:T(8,128)(2,1)S(1)} %multiply_convert_fusion.1, f32[1024,3,3,128]{0,3,2,1:T(8,128)} %bitcast.91, ...), kind=kOutput, calls=%fused_computation.95 | convolution fusion | flops 2461928448 | bytes 41709056 | tf_op jit(solution)/shard_map/sub | solution.py:102
  186.6 15.0 %fusion.26 = bf16[3,128,1024]{2,1,0:T(8,128)(2,1)S(1)} fusion(f32[3,1024,3072]{2,1,0:T(8,128)} %get-tuple-element.19, f32[3,1024]{1,0:T(4,128)} %get-tuple-element.18, bf16[1536,3,128]{0,2,1:T(8,128)(2,1)} %collective-permute-done, bf16[1024,3,128]{0,2,1:T(8,128)(2,1)} %copy-done.3, bf16[512,3,128]{0,2,1:T(8,128)(2,1)} %bitcast.93), kind=kOutput, calls=%fused_computation.42 | convolution fusion | flops 2442264576 | bytes 40906752 | tf_op jit(solution)/shard_map/hqk,khe->qhe/dot_general | solution.py:104
  201.7 8.1 %fusion.13 = f32[1024,3072]{1,0:T(8,128)} fusion(bf16[1024,384]{0,1:T(8,128)(2,1)S(1)} %bitcast.94, bf16[1536,3072]{1,0:T(8,128)(2,1)} %param.25, s32[]{:T(128)S(6)} %select_n.66), kind=kOutput, calls=%fused_computation.21 | convolution fusion | flops 2415919104 | bytes 15728644 | tf_op jit(solution)/shard_map/dot_general | solution.py:110
  211.2 113.8 %reduce-scatter.2.cloned.1.call-done = f32[256,3072]{1,0:T(8,128)} async-done(((f32[1024,3072]{1,0:T(8,128)}), f32[256,3072]{1,0:T(8,128)}) %reduce-scatter.2.cloned.1.call-update) | async-done | bytes 3145744 | tf_op jit(solution)/shard_map/reduce_scatter | solution.py:109
  325.0 2.3 fusion.47
  329.2 2.8 collective-permute-start.2
  334.0 1.9 subtract_bitcast_fusion
  (72 shorter events, 24.7 us)
Async XLA Ops:
  7.2 9.6 %copy-start = (bf16[64,3072]{1,0:T(8,128)(2,1)S(1)}, bf16[64,3072]{1,0:T(8,128)(2,1)}, u32[]{:S(2)}) copy-start(bf16[64,3072]{1,0:T(8,128)(2,1)} %param.20) | copy-start | bytes 1179652
  7.2 52.7 %all-gather.3.cloned.1.call-start = ((), (), s32[]{:S(2)}) async-start(), calls=%async_computation.1 | async-start | bytes 3932160 | tf_op jit(solution)/shard_map/all_gather | solution.py:70
  16.7 110.7 %all-gather.5.cloned.1.call-start = ((), (), s32[]{:S(2)}) async-start(), calls=%async_computation.2 | async-start | bytes 7864320 | tf_op jit(solution)/shard_map/all_gather | solution.py:69
  20.3 2.1 copy-start.8
  20.3 2.1 copy-start.9
  22.2 302.8 %reduce-scatter.2.cloned.1.call-start = ((), (), s32[]{:S(2)}) async-start(), calls=%async_computation.3 | async-start | bytes 15728640 | tf_op jit(solution)/shard_map/reduce_scatter | solution.py:109
  66.9 5.3 %copy-start.10 = (f32[128]{0:T(128)S(1)}, f32[128]{0:T(128)}, u32[]{:S(2)}) copy-start(f32[128]{0:T(128)} %param.24) | copy-start | bytes 1540
  138.8 2.2 copy-start.2
  149.0 0.9 copy-start.4
  151.0 16.0 %collective-permute-start.1 = (bf16[1536,3,128]{2,0,1:T(8,128)(2,1)}, bf16[1536,3,128]{2,0,1:T(8,128)(2,1)}, u32[]{:S(2)}, u32[]{:S(2)}) collective-permute-start(bf16[1536,3,128]{2,0,1:T(8,128)(2,1)} %pad_maximum_fusion.2), channel_id=1, source_target_pairs={{0,4},{4,0},{8,12},{12,8},{16,20},{20,16},{24,28},{28,24},{32,36},... | collective-permute-start | bytes 3538952 | tf_op jit(solution)/shard_map/ppermute | solution.py:12
  162.4 0.9 copy-start.3
  165.4 21.2 %collective-permute-start = (bf16[1536,3,128]{0,2,1:T(8,128)(2,1)}, bf16[1536,3,128]{0,2,1:T(8,128)(2,1)}, u32[]{:S(2)}, u32[]{:S(2)}) collective-permute-start(bf16[1536,3,128]{0,2,1:T(8,128)(2,1)} %pad_maximum_fusion.1), channel_id=1, source_target_pairs={{0,4},{4,0},{8,12},{12,8},{16,20},{20,16},{24,28},{28,24},{32,36},... | collective-permute-start | bytes 3538952 | tf_op jit(solution)/shard_map/ppermute | solution.py:12
  209.8 115.3 %copy-start.6 = (f32[1,1,3072]{2,0,1:T(1,128)S(1)}, f32[1,1,3072]{2,0,1:T(1,128)}, u32[]{:S(2)}) copy-start(f32[1,1,3072]{2,0,1:T(1,128)} %get-tuple-element.4) | copy-start | bytes 36868
  327.4 0.7 copy-start.7
  327.4 1.1 copy-start.11
  327.4 8.5 %copy-start.1 = (bf16[64,3072]{1,0:T(8,128)(2,1)S(1)}, bf16[64,3072]{1,0:T(8,128)(2,1)}, u32[]{:S(2)}) copy-start(bf16[64,3072]{1,0:T(8,128)(2,1)} %param.20) | copy-start | bytes 1179652
  327.4 5.3 %copy-start.12 = (f32[8]{0:T(128)S(1)}, f32[8]{0:T(128)}, u32[]{:S(2)}) copy-start(f32[8]{0:T(128)} %param.31) | copy-start | bytes 100
  327.4 6.0 %copy-start.13 = (f32[16]{0:T(128)S(1)}, f32[16]{0:T(128)}, u32[]{:S(2)}) copy-start(f32[16]{0:T(128)} %param.30) | copy-start | bytes 196
  327.4 6.6 %copy-start.5 = (f32[256,64]{0,1:T(8,128)S(1)}, f32[256,64]{0,1:T(8,128)}, u32[]{:S(2)}) copy-start(f32[256,64]{0,1:T(8,128)} %param.18) | copy-start | bytes 196612
  329.2 4.8 %collective-permute-start.2 = (bf16[256,64]{0,1:T(8,128)(2,1)S(1)}, bf16[256,64]{0,1:T(8,128)(2,1)S(1)}, u32[]{:S(2)}, u32[]{:S(2)}) collective-permute-start(bf16[256,64]{0,1:T(8,128)(2,1)S(1)} %get-tuple-element.20), channel_id=1, source_target_pairs={{0,64},{64,0},{1,65},{65,1},{2,66},{66,2},{3,67},{67,3},{4,68},{68... | collective-permute-start | bytes 98312 | tf_op jit(solution)/shard_map/ppermute | solution.py:12
Sparse Core Ops, SparseCore 0:
  16.8 42.9 all-gather.2
  61.5 65.8 all-gather.4
  209.9 115.0 reduce-scatter.1
where the time goes:
time: 343 us; the launch traced here: 342 us
  waiting for transfers between devices  204 us (59%)
  matrix products  63.3 us (18%)
  other arithmetic  27.7 us (8%)
  local copies, waits for them, and re-layouts  27.4 us (8%)
  between operations  16.7 us (5%)
  starting transfers between devices  3.83 us (1%)
    reduce_scatter x1, waiting for transfers between devices, local(): lax.psum_scatter(jnp.dot(mixed, w_local, preferred_element_type=jnp.float...  114 us
    all_gather x1, waiting for transfers between devices, local(): lax.all_gather(img_mod, 'mp', axis=0, tiled=True)  55 us
    all_gather x1, waiting for transfers between devices, local(): lax.all_gather(txt_mod, 'mp', axis=0, tiled=True)  34.8 us
    sub x1, matrix products, local(): weights = jnp.exp(scores - jnp.max(scores, -1, keepdims=True))  19.6 us
    dot_general x1, matrix products, local(): jnp.einsum('hqk,khe->qhe', probs, all_values, preferred_element_type=jnp....  15 us
    dot_general x1, matrix products, local(): jnp.dot(img_full, w_img_qkv, preferred_element_type=jnp.float32)  11.3 us
    unnamed x30, local copies, waits for them, and re-layouts  10.4 us
    dot_general x1, matrix products, local(): jnp.dot(mixed, w_local, preferred_element_type=jnp.float32)  8.09 us
  transfers between devices with their start and end apart: 6, of which 3 were waited for; matrix products, arithmetic and copies ran while one was open for 17% of the time, Pallas kernels for 0%

commit v1 on v0

--- a/solution.py
+++ b/solution.py
@@ -4,6 +4,18 @@
 from jax.sharding import PartitionSpec as P
 
 HD = 128
+
+
+def _check_heaps(load):
+    mesh_ax = "mp"
+    extent = lax.axis_size(mesh_ax)
+    return lax.all_to_all(
+        jnp.tile(load, list(map(lambda num: extent if num == 0 else 1, range(load.ndim)))),
+        axis_name=mesh_ax,
+        split_axis=0,
+        concat_axis=0,
+        tiled=True,
+    )
 
 
 def partner(value, axis, bit):
@@ -65,10 +77,7 @@
     txt_mod = (
         layer_norm(text_hidden[0].astype(jnp.float32)) * (1.0 + text_rows[1]) + text_rows[0]
     ).astype(jnp.bfloat16)
-    img_full, txt_full = (
-        lax.all_gather(img_mod, "mp", axis=0, tiled=True),
-        lax.all_gather(txt_mod, "mp", axis=0, tiled=True),
-    )
+    img_full, txt_full = (lax.all_gather(img_mod, "mp", axis=0, tiled=True), _check_heaps(txt_mod))
     qkv = jnp.dot(img_full, w_img_qkv, preferred_element_type=jnp.float32).reshape(
         full_img, local_heads, 3, HD
     )

time: 343 us -> 329 us (0.959)
  waiting for transfers between devices: 204 us -> 183 us
  starting transfers between devices: 3.83 us -> 9.21 us
    all_to_all x0 -> x1, waiting for transfers between devices: none -> 56.4 us  [_check_heaps(): lax.all_to_all(jnp.tile(load, list(map(lambda num: extent if num == 0 els...]
    all_gather x1, waiting for transfers between devices: 55 us -> 13.7 us  [local(): lax.all_gather(img_mod, 'mp', axis=0, tiled=True)]
    all_gather x1 -> x0, waiting for transfers between devices: 34.8 us -> none  [local(): lax.all_gather(txt_mod, 'mp', axis=0, tiled=True)]
    dot_general x0 -> x1, local copies, waits for them, and re-layouts: none -> 7 us  [local(): jnp.dot(txt_full, w_txt_kv, preferred_element_type=jnp.float32)]
    all_to_all x0 -> x1, starting transfers between devices: none -> 5.85 us  [_check_heaps(): lax.all_to_all(jnp.tile(load, list(map(lambda num: extent if num == 0 els...]
    slice x2 -> x0, local copies, waits for them, and re-layouts: 5.24 us -> none  [the longest x1 3.13 us: local(): value_txt = text_kv[:, :, 1].astype(jnp.bfloat16)]
    convert_element_type x0 -> x2, local copies, waits for them, and re-layouts: none -> 3.87 us  [local(): value_txt = text_kv[:, :, 1].astype(jnp.bfloat16)]
    unnamed x30 -> x33, local copies, waits for them, and re-layouts: 10.4 us -> 8.42 us
where the time goes in v1:
time: 329 us; the launch traced here: 327 us
  waiting for transfers between devices  183 us (56%)
  matrix products  62.6 us (19%)
  local copies, waits for them, and re-layouts  28.8 us (9%)
  other arithmetic  26.7 us (8%)
  between operations  17 us (5%)
  starting transfers between devices  9.21 us (3%)
    reduce_scatter x1, waiting for transfers between devices, local(): lax.psum_scatter(jnp.dot(mixed, w_local, preferred_element_type=jnp.float...  113 us
    all_to_all x1, waiting for transfers between devices, _check_heaps(): lax.all_to_all(jnp.tile(load, list(map(lambda num: extent if num == 0 els...  56.4 us
    sub x1, matrix products, local(): weights = jnp.exp(scores - jnp.max(scores, -1, keepdims=True))  19.6 us
    dot_general x1, matrix products, local(): jnp.einsum('hqk,khe->qhe', probs, all_values, preferred_element_type=jnp....  15 us
    all_gather x1, waiting for transfers between devices, local(): lax.all_gather(img_mod, 'mp', axis=0, tiled=True)  13.7 us
    dot_general x1, matrix products, local(): jnp.dot(img_full, w_img_qkv, preferred_element_type=jnp.float32)  11.3 us
    unnamed x33, local copies, waits for them, and re-layouts  8.42 us
    dot_general x1, matrix products, local(): jnp.dot(mixed, w_local, preferred_element_type=jnp.float32)  8.09 us
  transfers between devices with their start and end apart: 6, of which 3 were waited for; matrix products, arithmetic and copies ran while one was open for 17% of the time, Pallas kernels for 0%

profile of v1, /device:TPU:1, one launch (start us, length us, event | category | flops | bytes accessed | tf_op | source)
XLA Modules:
  0.0 327.4 jit_solution(13361720315793575944)
XLA Ops:
  14.4 1.9 add_convert_fusion.1
  19.1 1.5 fusion.21
  20.7 2.0 tile.2
  22.7 5.8 %all-to-all-start = ((bf16[4,128,3072]{2,1,0:T(8,128)(2,1)}), bf16[4,128,3072]{2,1,0:T(8,128)(2,1)}, u32[]{:S(2)}, u32[]{:S(2)}) async-start(bf16[4,128,3072]{2,1,0:T(8,128)(2,1)} %tile.2), calls=%async_computation | async-start | bytes 6291456 | tf_op jit(solution)/shard_map/all_to_all | solution.py:12
  28.6 7.0 %copy.38 = bf16[768,3072]{1,0:T(8,128)(2,1)} copy(bf16[768,3072]{0,1:T(8,128)(2,1)} %bitcast.94) | data formatting | bytes 9437184 | tf_op jit(solution)/shard_map/dot_general | solution.py:87
  40.1 56.4 %all-to-all-done = bf16[4,128,3072]{2,1,0:T(8,128)(2,1)} async-done(((bf16[4,128,3072]{2,1,0:T(8,128)(2,1)}), bf16[4,128,3072]{2,1,0:T(8,128)(2,1)}, u32[]{:S(2)}, u32[]{:S(2)}) %all-to-all-start) | async-done | bytes 3145760 | tf_op jit(solution)/shard_map/all_to_all | solution.py:12
  96.5 6.3 %fusion.54 = f32[512,3,2,128]{3,0,2,1:T(8,128)S(1)} fusion(bf16[512,3072,1,1]{1,0,3,2:T(8,128)(2,1)} %bitcast.8, bf16[3,2,128,3072]{3,2,1,0:T(8,128)(2,1)} %bitcast.95), kind=kOutput, calls=%fused_computation.98 | convolution fusion | flops 2415919104 | bytes 9437184 | tf_op jit(solution)/shard_map/dot_general | solution.py:87
  104.2 13.7 %all-gather.2.cloned.1.call-done = bf16[1024,3072]{1,0:T(8,128)(2,1)} async-done(((bf16[256,3072]{1,0:T(8,128)(2,1)}), bf16[1024,3072]{1,0:T(8,128)(2,1)}) %all-gather.2.cloned.1.call-update) | async-done | bytes 6291472 | tf_op jit(solution)/shard_map/all_gather | solution.py:80
  117.9 11.3 %fusion.55 = f32[1024,1152]{0,1:T(8,128)S(1)} fusion(bf16[1024,3072]{1,0:T(8,128)(2,1)} %all-gather.2.cloned.1.call-done, bf16[3072,1152]{1,0:T(8,128)(2,1)} %param.21), kind=kOutput, calls=%fused_computation.99 | convolution fusion | flops 7247757312 | bytes 18087936 | tf_op jit(solution)/shard_map/dot_general | solution.py:81
  129.2 2.1 copy-done.2
  132.6 3.0 copy.43
  135.6 1.9 fusion.22
  137.5 1.9 fusion.24
  141.9 1.9 fusion.31
  143.8 1.9 copy.32
  148.2 2.1 pad_maximum_fusion.1
  150.4 1.6 multiply_reduce_fusion.2
  152.6 19.6 %fusion.52 = (f32[3,1024]{1,0:T(4,128)}, f32[3,1024,3072]{2,1,0:T(8,128)}) fusion(pred[3072]{0:T(1024)(128)(4,1)S(1)} %pad_add_fusion, bf16[1536,3,128]{2,0,1:T(8,128)(2,1)} %collective-permute-done.1, bf16[1024,3,128]{2,0,1:T(8,128)(2,1)} %copy-done.4, bf16[512,3,128]{2,0,1:T(8,128)(2,1)S(1)} %multiply_convert_fusion.1, f32[1024,3,3,128]{0,3,2,1:T(8,128)} %bitcast.99, ...), kind=kOutput, calls=%fused_computation.96 | convolution fusion | flops 2461928448 | bytes 41713152 | tf_op jit(solution)/shard_map/sub | solution.py:111
  172.2 15.0 %fusion.26 = bf16[3,128,1024]{2,1,0:T(8,128)(2,1)S(1)} fusion(f32[3,1024,3072]{2,1,0:T(8,128)} %get-tuple-element.19, f32[3,1024]{1,0:T(4,128)} %get-tuple-element.18, bf16[1536,3,128]{0,2,1:T(8,128)(2,1)} %collective-permute-done, bf16[1024,3,128]{0,2,1:T(8,128)(2,1)} %copy-done.3, bf16[512,3,128]{0,2,1:T(8,128)(2,1)} %copy.32), kind=kOutput, calls=%fused_computation.42 | convolution fusion | flops 2442264576 | bytes 40906752 | tf_op jit(solution)/shard_map/hqk,khe->qhe/dot_general | solution.py:113
  187.2 8.1 %fusion.13 = f32[1024,3072]{1,0:T(8,128)} fusion(bf16[1024,384]{0,1:T(8,128)(2,1)S(1)} %bitcast.100, bf16[1536,3072]{1,0:T(8,128)(2,1)} %param.25, s32[]{:T(128)S(6)} %select_n.66), kind=kOutput, calls=%fused_computation.21 | convolution fusion | flops 2415919104 | bytes 15728644 | tf_op jit(solution)/shard_map/dot_general | solution.py:119
  196.8 113.1 %reduce-scatter.2.cloned.1.call-done = f32[256,3072]{1,0:T(8,128)} async-done(((f32[1024,3072]{1,0:T(8,128)}), f32[256,3072]{1,0:T(8,128)}) %reduce-scatter.2.cloned.1.call-update) | async-done | bytes 3145744 | tf_op jit(solution)/shard_map/reduce_scatter | solution.py:118
  309.9 2.3 fusion.48
  314.0 2.8 collective-permute-start.2
  318.8 1.8 subtract_bitcast_fusion
  (75 shorter events, 25.3 us)
Async XLA Ops:
  7.2 2.6 copy-start
  7.2 110.7 %all-gather.2.cloned.1.call-start = ((), (), s32[]{:S(2)}) async-start(), calls=%async_computation.2 | async-start | bytes 7864320 | tf_op jit(solution)/shard_map/all_gather | solution.py:80
  22.7 73.8 %all-to-all-start = ((bf16[4,128,3072]{2,1,0:T(8,128)(2,1)}), bf16[4,128,3072]{2,1,0:T(8,128)(2,1)}, u32[]{:S(2)}, u32[]{:S(2)}) async-start(bf16[4,128,3072]{2,1,0:T(8,128)(2,1)} %tile.2), calls=%async_computation | async-start | bytes 6291456 | tf_op jit(solution)/shard_map/all_to_all | solution.py:12
  28.5 281.3 %reduce-scatter.2.cloned.1.call-start = ((), (), s32[]{:S(2)}) async-start(), calls=%async_computation.3 | async-start | bytes 15728640 | tf_op jit(solution)/shard_map/reduce_scatter | solution.py:118
  28.5 7.0 %copy-start.12 = (s32[2,16]{1,0:T(2,128)S(1)}, s32[2,16]{1,0:T(2,128)}, u32[]{:S(2)}) copy-start(s32[2,16]{1,0:T(2,128)} %param.34) | copy-start | bytes 388
  28.5 8.3 %copy-start.9 = (s32[16]{0:T(128)S(1)}, s32[16]{0:T(128)}, u32[]{:S(2)}) copy-start(s32[16]{0:T(128)} %param.33) | copy-start | bytes 196
  28.5 8.3 %copy-start.10 = (s32[16]{0:T(128)S(1)}, s32[16]{0:T(128)}, u32[]{:S(2)}) copy-start(s32[16]{0:T(128)} %param.32) | copy-start | bytes 196
  96.5 7.4 %copy-start.11 = (f32[128]{0:T(128)S(1)}, f32[128]{0:T(128)}, u32[]{:S(2)}) copy-start(f32[128]{0:T(128)} %param.24) | copy-start | bytes 1540
  102.8 1.1 copy-start.5
  129.2 2.1 copy-start.2
  139.4 0.9 copy-start.4
  141.4 11.1 %collective-permute-start.1 = (bf16[1536,3,128]{2,0,1:T(8,128)(2,1)}, bf16[1536,3,128]{2,0,1:T(8,128)(2,1)}, u32[]{:S(2)}, u32[]{:S(2)}) collective-permute-start(bf16[1536,3,128]{2,0,1:T(8,128)(2,1)} %pad_maximum_fusion.2), channel_id=1, source_target_pairs={{0,4},{4,0},{8,12},{12,8},{16,20},{20,16},{24,28},{28,24},{32,36},... | collective-permute-start | bytes 3538952 | tf_op jit(solution)/shard_map/ppermute | solution.py:24
  147.3 0.9 copy-start.3
  150.3 21.9 %collective-permute-start = (bf16[1536,3,128]{0,2,1:T(8,128)(2,1)}, bf16[1536,3,128]{0,2,1:T(8,128)(2,1)}, u32[]{:S(2)}, u32[]{:S(2)}) collective-permute-start(bf16[1536,3,128]{0,2,1:T(8,128)(2,1)} %pad_maximum_fusion.1), channel_id=1, source_target_pairs={{0,4},{4,0},{8,12},{12,8},{16,20},{20,16},{24,28},{28,24},{32,36},... | collective-permute-start | bytes 3538952 | tf_op jit(solution)/shard_map/ppermute | solution.py:24
  312.2 0.7 copy-start.7
  312.2 0.7 copy-start.8
  312.2 1.1 copy-start.13
  312.2 8.4 %copy-start.1 = (bf16[64,3072]{1,0:T(8,128)(2,1)S(1)}, bf16[64,3072]{1,0:T(8,128)(2,1)}, u32[]{:S(2)}) copy-start(bf16[64,3072]{1,0:T(8,128)(2,1)} %param.20) | copy-start | bytes 1179652
  312.2 5.3 %copy-start.14 = (f32[8]{0:T(128)S(1)}, f32[8]{0:T(128)}, u32[]{:S(2)}) copy-start(f32[8]{0:T(128)} %param.31) | copy-start | bytes 100
  312.3 5.9 %copy-start.15 = (f32[16]{0:T(128)S(1)}, f32[16]{0:T(128)}, u32[]{:S(2)}) copy-start(f32[16]{0:T(128)} %param.30) | copy-start | bytes 196
  312.3 6.5 %copy-start.6 = (f32[256,64]{0,1:T(8,128)S(1)}, f32[256,64]{0,1:T(8,128)}, u32[]{:S(2)}) copy-start(f32[256,64]{0,1:T(8,128)} %param.18) | copy-start | bytes 196612
  314.0 4.7 %collective-permute-start.2 = (bf16[256,64]{0,1:T(8,128)(2,1)S(1)}, bf16[256,64]{0,1:T(8,128)(2,1)S(1)}, u32[]{:S(2)}, u32[]{:S(2)}) collective-permute-start(bf16[256,64]{0,1:T(8,128)(2,1)S(1)} %get-tuple-element.20), channel_id=1, source_target_pairs={{0,64},{64,0},{1,65},{65,1},{2,66},{66,2},{3,67},{67,3},{4,68},{68... | collective-permute-start | bytes 98312 | tf_op jit(solution)/shard_map/ppermute | solution.py:24
Sparse Core Ops, SparseCore 0:
  16.4 101.4 all-gather.1
  195.4 114.3 reduce-scatter.1
